TPU v7x, 512 devices: a whole 4x8x8 slice. The times are simulated.
512 devices in a mesh: rows: 64 (over x, z, core), cols: 8 (over y).
Axes of the slice: x: 4, y: 8, z: 8, core: 2. Of those that a mesh axis runs over, the one named last changes fastest.
Arguments:
- right_sides: float32 [4, 64, 128, 256], P(None, 'rows'), may hold values from -6 to 6
- factor_blocks: bfloat16 [3, 64, 8, 8, 256, 256], P(None, 'rows', 'cols'), may hold values from -0.125 to 0.125
- diag_inverses: bfloat16 [4, 64, 256, 256], P(None, 'rows')
- source_ids: int32 [3, 64, 8, 8], P(None, 'rows', 'cols'), may hold values from 0 to 191, as said below
- block_counts: int32 [3, 64, 8], P(None, 'rows', 'cols'), may hold values from 1 to 8, as said below
Outputs:
- solution: float32 [4, 64, 128, 256], P(None, 'rows', 'cols')
Inputs may be any that keep to these rules, and one draw needn't show every extreme that they name: source_ids[l, t, c, k] = m * 64 + s names a supernode of a level m <= l with s % 8 == c. block_counts[l, t, c] slots of target t on group c hold blocks of the factor; slots at and past it are not part of the factor. In every level some target and group has all 8 slots live.
All inputs are finite; a program needn't handle non-finite values.
Results may differ from a plain program's by a relative error of at most 0.007.
Values may be sent and summed in bfloat16 or wider, within the bound.
A program may use at most 128 MiB of HBM per device.

v0:
```python
import jax
import jax.numpy as jnp
from jax import lax
from jax.sharding import PartitionSpec as P


def locate(source, row_count, col_count):
    return source // row_count * (row_count // col_count) + source % row_count // col_count


def slot_sum(running, blocks, chosen_ids, live_count, solved_store, row_count, col_count):

    def add_block(slot_index, partial_value):
        source = chosen_ids[slot_index]
        solved_piece = lax.dynamic_index_in_dim(
            solved_store, locate(source, row_count, col_count), 0, keepdims=False
        )
        factor_piece = lax.dynamic_index_in_dim(blocks, slot_index, 0, keepdims=False)
        return partial_value + jnp.dot(
            solved_piece, factor_piece, preferred_element_type=jnp.float32
        )

    return lax.fori_loop(0, live_count, add_block, running)


def shards(right_sides, factor_blocks, diag_inverses, source_ids, block_counts):
    row_count = lax.axis_size("rows")
    col_count = lax.axis_size("cols")
    level_count = right_sides.shape[0]
    rhs_count = right_sides.shape[2]
    block_width = right_sides.shape[3]
    share_rows = rhs_count // col_count
    col_index = lax.axis_index("cols")
    per_level = row_count // col_count
    solved_store = jnp.zeros(((level_count - 1) * per_level, rhs_count, block_width), jnp.bfloat16)
    partials = [jnp.zeros((rhs_count, block_width), jnp.float32)] * level_count
    solutions = []
    for level_index in range(level_count):
        if level_index > 0:
            partials[level_index] = slot_sum(
                partials[level_index],
                factor_blocks[level_index - 1, 0, 0],
                source_ids[level_index - 1, 0, 0],
                block_counts[level_index - 1, 0, 0],
                solved_store,
                row_count,
                col_count,
            )
        own_rhs = lax.dynamic_slice_in_dim(
            right_sides[level_index, 0], col_index * share_rows, share_rows, 0
        )
        if level_index > 0:
            own_rhs = own_rhs - lax.psum_scatter(
                partials[level_index], "cols", scatter_dimension=0, tiled=True
            )
        own_solution = jnp.dot(
            own_rhs.astype(jnp.bfloat16),
            diag_inverses[level_index, 0],
            preferred_element_type=jnp.float32,
        )
        solutions.append(own_solution)
        if level_index < level_count - 1:
            pieces = lax.all_gather(
                own_solution.astype(jnp.bfloat16)[None], "rows", axis=0, tiled=True
            )
            grouped = pieces.reshape(per_level, col_count, share_rows, block_width)
            regrouped = lax.all_to_all(grouped, "cols", split_axis=1, concat_axis=2, tiled=True)
            solved_store = solved_store.at[
                level_index * per_level : (level_index + 1) * per_level
            ].set(regrouped[:, 0])
    return jnp.stack(solutions)[:, None]


def solution(mesh):
    return jax.shard_map(
        shards,
        mesh=mesh,
        in_specs=(
            P(None, "rows", None, None),
            P(None, "rows", "cols", None, None, None),
            P(None, "rows", None, None),
            P(None, "rows", "cols", None),
            P(None, "rows", "cols"),
        ),
        out_specs=P(None, "rows", "cols", None),
        check_vma=False,
    )
```

profile of v0, /device:TPU:2, one launch (start us, length us, event | category | flops | bytes accessed | tf_op | source)
XLA Modules:
  0.0 462.0 jit_solution(18360709935676070336)
XLA Ops:
  6.5 0.9 slice.116
  7.5 1.0 fusion.40
  8.5 56.0 %all-gather = bf16[1024,256]{1,0:T(8,128)(2,1)S(1)} all-gather(bf16[16,256]{1,0:T(8,128)(2,1)S(1)} %get-tuple-element.425), channel_id=2, replica_groups=mesh['rows'=64,'cols'=8] {'rows'}, dimensions={0}, use_global_device_ids=true | all-gather | bytes 532480 | tf_op jit(solution)/shard_map/all_gather | solution.py:63
  64.5 0.8 copy.11
  65.4 7.1 %all-to-all-start = ((bf16[8,8,16,256]{3,2,0,1:T(8,128)(2,1)}), bf16[8,8,16,256]{3,2,0,1:T(8,128)(2,1)S(1)}, u32[]{:S(2)}, u32[]{:S(2)}) async-start(bf16[8,8,16,256]{3,2,0,1:T(8,128)(2,1)} %copy.11), calls=%async_computation | async-start | bytes 1048576 | tf_op jit(solution)/shard_map/all_to_all | solution.py:67
  72.5 0.6 fusion.39
  73.1 0.6 slice_bitcast_fusion.4
  73.7 3.5 slice_bitcast_fusion
  77.2 13.3 %all-to-all-done = bf16[8,8,16,256]{3,2,0,1:T(8,128)(2,1)S(1)} async-done(((bf16[8,8,16,256]{3,2,0,1:T(8,128)(2,1)}), bf16[8,8,16,256]{3,2,0,1:T(8,128)(2,1)S(1)}, u32[]{:S(2)}, u32[]{:S(2)}) %all-to-all-start) | async-done | bytes 524320 | tf_op jit(solution)/shard_map/all_to_all | solution.py:67
  90.7 21.3 %while.42 = (s32[]{:T(128)}, f32[128,256]{1,0:T(8,128)S(1)}, s32[]{:T(128)}, s32[8]{0:T(128)S(1)}, bf16[24,128,256]{2,1,0:T(8,128)(2,1)S(1)}, /*index=5*/bf16[8,...) while((s32[]{:T(128)}, f32[128,256]{1,0:T(8,128)S(1)}, ...), condition=%wide.region_1.2_spmd, body=%wide.region_0.0_spmd.sunk | while | flops 16810028 | bytes 459350 | solution.py:23
  91.4 0.7 dynamic_slice.141
  94.8 1.1 convolution_add_fusion.6
  96.5 0.7 dynamic_slice.141
  100.0 1.1 convolution_add_fusion.6
  101.7 0.7 dynamic_slice.141
  105.2 1.1 convolution_add_fusion.6
  106.8 0.7 dynamic_slice.141
  110.3 1.1 convolution_add_fusion.6
  112.0 0.7 copy-done.1
  112.7 51.3 %reduce-scatter.4.cloned.1.call-done = f32[16,256]{1,0:T(8,128)} async-done(((f32[128,256]{1,0:T(8,128)}), f32[16,256]{1,0:T(8,128)}) %reduce-scatter.4.cloned.1.call-update) | async-done | bytes 16400 | tf_op jit(solution)/shard_map/reduce_scatter | solution.py:53
  164.0 1.1 fusion.41
  165.0 50.9 %all-gather.1 = bf16[1024,256]{1,0:T(8,128)(2,1)S(1)} all-gather(bf16[16,256]{1,0:T(8,128)(2,1)S(1)} %get-tuple-element.427), channel_id=3, replica_groups=mesh['rows'=64,'cols'=8] {'rows'}, dimensions={0}, use_global_device_ids=true | all-gather | bytes 532480 | tf_op jit(solution)/shard_map/all_gather | solution.py:63
  215.9 0.8 copy.13
  216.7 4.6 all-to-all-start.1
  221.4 18.0 %all-to-all-done.1 = bf16[8,8,16,256]{3,2,0,1:T(8,128)(2,1)S(1)} async-done(((bf16[8,8,16,256]{3,2,0,1:T(8,128)(2,1)}), bf16[8,8,16,256]{3,2,0,1:T(8,128)(2,1)S(1)}, u32[]{:S(2)}, u32[]{:S(2)}) %all-to-all-start.1) | async-done | bytes 524320 | tf_op jit(solution)/shard_map/all_to_all | solution.py:67
  239.4 15.6 %while.43 = (s32[]{:T(128)}, f32[128,256]{1,0:T(8,128)S(1)}, s32[]{:T(128)}, s32[8]{0:T(128)S(1)}, bf16[24,128,256]{2,1,0:T(8,128)(2,1)S(1)}, /*index=5*/bf16[8,...) while((s32[]{:T(128)}, f32[128,256]{1,0:T(8,128)S(1)}, ...), condition=%wide.region_4.5_spmd, body=%wide.region_3.4_spmd.sunk | while | flops 16810028 | bytes 459350 | solution.py:23
  240.1 0.7 dynamic_slice.144
  243.3 1.1 convolution_add_fusion.7
  245.1 0.7 dynamic_slice.144
  248.3 1.1 convolution_add_fusion.7
  250.1 0.7 dynamic_slice.144
  253.3 1.1 convolution_add_fusion.7
  255.1 0.6 copy-done.2
  255.7 57.3 %reduce-scatter.6.cloned.1.call-done = f32[16,256]{1,0:T(8,128)} async-done(((f32[128,256]{1,0:T(8,128)}), f32[16,256]{1,0:T(8,128)}) %reduce-scatter.6.cloned.1.call-update) | async-done | bytes 16400 | tf_op jit(solution)/shard_map/reduce_scatter | solution.py:53
  313.1 1.1 fusion.42
  314.1 50.8 %all-gather.2 = bf16[1024,256]{1,0:T(8,128)(2,1)S(1)} all-gather(bf16[16,256]{1,0:T(8,128)(2,1)S(1)} %get-tuple-element.429), channel_id=4, replica_groups=mesh['rows'=64,'cols'=8] {'rows'}, dimensions={0}, use_global_device_ids=true | all-gather | bytes 532480 | tf_op jit(solution)/shard_map/all_gather | solution.py:63
  364.9 0.9 copy.15
  365.8 4.6 %all-to-all-start.2 = ((bf16[8,8,16,256]{3,2,0,1:T(8,128)(2,1)}), bf16[8,8,16,256]{3,2,0,1:T(8,128)(2,1)S(1)}, u32[]{:S(2)}, u32[]{:S(2)}) async-start(bf16[8,8,16,256]{3,2,0,1:T(8,128)(2,1)} %copy.15), calls=%async_computation.4 | async-start | bytes 1048576 | tf_op jit(solution)/shard_map/all_to_all | solution.py:67
  370.5 18.0 %all-to-all-done.2 = bf16[8,8,16,256]{3,2,0,1:T(8,128)(2,1)S(1)} async-done(((bf16[8,8,16,256]{3,2,0,1:T(8,128)(2,1)}), bf16[8,8,16,256]{3,2,0,1:T(8,128)(2,1)S(1)}, u32[]{:S(2)}, u32[]{:S(2)}) %all-to-all-start.2) | async-done | bytes 524320 | tf_op jit(solution)/shard_map/all_to_all | solution.py:67
  388.6 12.5 %while.44 = (s32[]{:T(128)}, f32[128,256]{1,0:T(8,128)S(1)}, s32[]{:T(128)}, s32[8]{0:T(128)S(1)}, bf16[24,128,256]{2,1,0:T(8,128)(2,1)S(1)}, /*index=5*/bf16[8,...) while((s32[]{:T(128)}, f32[128,256]{1,0:T(8,128)S(1)}, ...), condition=%wide.region_7.8_spmd, body=%wide.region_6.7_spmd.sunk | while | flops 16810028 | bytes 459350 | solution.py:23
  389.2 0.6 dynamic_slice.147
  393.2 0.6 dynamic_slice.147
  396.3 0.2 convolution_add_fusion.8
  397.2 0.6 dynamic_slice.147
  401.1 0.6 copy-done
  401.8 51.9 %reduce-scatter.8.cloned.1.call-done = f32[16,256]{1,0:T(8,128)} async-done(((f32[128,256]{1,0:T(8,128)}), f32[16,256]{1,0:T(8,128)}) %reduce-scatter.8.cloned.1.call-update) | async-done | bytes 16400 | tf_op jit(solution)/shard_map/reduce_scatter | solution.py:53
  453.7 1.1 convolution_bitcast_fusion
  454.8 0.6 maximum_bitcast_fusion
  (31 shorter events, 0.9 us)
Async XLA Ops:
  6.5 66.0 %copy-start.4 = (s32[3,1,1]{0,2,1:T(1,128)S(1)}, s32[3,1,1]{0,2,1:T(1,128)}, u32[]{:S(2)}) copy-start(s32[3,1,1]{0,2,1:T(1,128)} %param.21) | copy-start | bytes 40
  6.5 66.6 %copy-start.5 = (s32[3,1,1,8]{3,2,1,0:T(1,128)S(1)}, s32[3,1,1,8]{3,2,1,0:T(1,128)}, u32[]{:S(2)}) copy-start(s32[3,1,1,8]{3,2,1,0:T(1,128)} %param.20) | copy-start | bytes 292
  65.4 25.1 %all-to-all-start = ((bf16[8,8,16,256]{3,2,0,1:T(8,128)(2,1)}), bf16[8,8,16,256]{3,2,0,1:T(8,128)(2,1)S(1)}, u32[]{:S(2)}, u32[]{:S(2)}) async-start(bf16[8,8,16,256]{3,2,0,1:T(8,128)(2,1)} %copy.11), calls=%async_computation | async-start | bytes 1048576 | tf_op jit(solution)/shard_map/all_to_all | solution.py:67
  72.5 91.5 %reduce-scatter.4.cloned.1.call-start = ((), (), s32[]{:S(2)}) async-start(), calls=%async_computation.6 | async-start | bytes 147456 | tf_op jit(solution)/shard_map/reduce_scatter | solution.py:53
  90.7 22.0 %copy-start.3 = (f32[4,1,128,256]{3,2,1,0:T(8,128)S(1)}, f32[4,1,128,256]{3,2,1,0:T(8,128)}, u32[]{:S(2)}) copy-start(f32[4,1,128,256]{3,2,1,0:T(8,128)} %param.17) | copy-start | bytes 1572868
  112.0 0.7 copy-start.1
  216.7 22.7 %copy-start.7 = (s32[8]{0:T(128)S(1)}, s32[8]{0:T(128)}, u32[]{:S(2)}) copy-start(s32[8]{0:T(128)} %get-tuple-element.596) | copy-start | bytes 100
  216.7 22.6 %all-to-all-start.1 = ((bf16[8,8,16,256]{3,2,0,1:T(8,128)(2,1)}), bf16[8,8,16,256]{3,2,0,1:T(8,128)(2,1)S(1)}, u32[]{:S(2)}, u32[]{:S(2)}) async-start(bf16[8,8,16,256]{3,2,0,1:T(8,128)(2,1)} %copy.13), calls=%async_computation.2 | async-start | bytes 1048576 | tf_op jit(solution)/shard_map/all_to_all | solution.py:67
  221.3 91.8 %reduce-scatter.6.cloned.1.call-start = ((), (), s32[]{:S(2)}) async-start(), calls=%async_computation.7 | async-start | bytes 147456 | tf_op jit(solution)/shard_map/reduce_scatter | solution.py:53
  255.1 0.6 copy-start.2
  365.8 22.8 %copy-start.6 = (s32[8]{0:T(128)S(1)}, s32[8]{0:T(128)}, u32[]{:S(2)}) copy-start(s32[8]{0:T(128)} %get-tuple-element.644) | copy-start | bytes 100
  365.8 22.6 %all-to-all-start.2 = ((bf16[8,8,16,256]{3,2,0,1:T(8,128)(2,1)}), bf16[8,8,16,256]{3,2,0,1:T(8,128)(2,1)S(1)}, u32[]{:S(2)}, u32[]{:S(2)}) async-start(bf16[8,8,16,256]{3,2,0,1:T(8,128)(2,1)} %copy.15), calls=%async_computation.4 | async-start | bytes 1048576 | tf_op jit(solution)/shard_map/all_to_all | solution.py:67
  370.4 83.3 %reduce-scatter.8.cloned.1.call-start = ((), (), s32[]{:S(2)}) async-start(), calls=%async_computation.8 | async-start | bytes 147456 | tf_op jit(solution)/shard_map/reduce_scatter | solution.py:53
  401.1 0.6 copy-start
Sparse Core Ops, SparseCore 0:
  112.8 51.1 reduce-scatter.3
  255.9 57.1 reduce-scatter.5
  401.9 51.7 reduce-scatter.7
where the time goes:
time: 464 us; the launch traced here: 462 us
  waiting for transfers between devices  210 us (45%)
  blocking collectives  158 us (34%)
  loops' own time  34.9 us (8%)
  local copies, waits for them, and re-layouts  16.9 us (4%)
  starting transfers between devices  16.4 us (4%)
  between operations  13.3 us (3%)
  matrix products  12.3 us (3%)
    reduce_scatter x3, waiting for transfers between devices, shards(): lax.psum_scatter(partials[level_index], 'cols', scatter_dimension=0, tile...  161 us
    all_gather x3, blocking collectives, shards(): lax.all_gather(own_solution.astype(jnp.bfloat16)[None], 'rows', axis=0, t...  158 us
    all_to_all x3, waiting for transfers between devices, shards(): lax.all_to_all(grouped, 'cols', split_axis=1, concat_axis=2, tiled=True)  49.2 us
    another operation x3, loops' own time, slot_sum(): return lax.fori_loop(0, live_count, add_block, running)  34.9 us
    all_to_all x3, starting transfers between devices, shards(): lax.all_to_all(grouped, 'cols', split_axis=1, concat_axis=2, tiled=True)  16.3 us
  transfers between devices with their start and end apart: 6, of which 6 were waited for; matrix products, arithmetic and copies ran while one was open for 1% of the time, Pallas kernels for 0%

commit v1 on v0

--- a/solution.py
+++ b/solution.py
@@ -60,8 +60,14 @@
         )
         solutions.append(own_solution)
         if level_index < level_count - 1:
-            pieces = lax.all_gather(
-                own_solution.astype(jnp.bfloat16)[None], "rows", axis=0, tiled=True
+            pieces = jnp.concatenate(
+                lax.all_to_all(
+                    jnp.stack([own_solution.astype(jnp.bfloat16)[None]] * lax.axis_size("rows")),
+                    "rows",
+                    0,
+                    0,
+                ),
+                axis=0,
             )
             grouped = pieces.reshape(per_level, col_count, share_rows, block_width)
             regrouped = lax.all_to_all(grouped, "cols", split_axis=1, concat_axis=2, tiled=True)

time: 464 us -> 396 us (0.85)
  blocking collectives: 158 us -> 85.5 us
    all_gather x3 -> x0, blocking collectives: 158 us -> none  [shards(): lax.all_gather(own_solution.astype(jnp.bfloat16)[None], 'rows', axis=0, t...]
    all_to_all x0 -> x3, blocking collectives: none -> 85.5 us  [shards(): lax.all_to_all(jnp.stack([own_solution.astype(jnp.bfloat16)[None]] * lax....]
where the time goes in v1:
time: 396 us; the launch traced here: 394 us
  waiting for transfers between devices  214 us (54%)
  blocking collectives  85.5 us (22%)
  loops' own time  34.2 us (9%)
  starting transfers between devices  16.1 us (4%)
  local copies, waits for them, and re-layouts  15.5 us (4%)
  matrix products  14.4 us (4%)
  between operations  13.3 us (3%)
    reduce_scatter x3, waiting for transfers between devices, shards(): lax.psum_scatter(partials[level_index], 'cols', scatter_dimension=0, tile...  161 us
    all_to_all x3, blocking collectives, shards(): lax.all_to_all(jnp.stack([own_solution.astype(jnp.bfloat16)[None]] * lax....  85.5 us
    all_to_all x3, waiting for transfers between devices, shards(): lax.all_to_all(grouped, 'cols', split_axis=1, concat_axis=2, tiled=True)  52.5 us
    another operation x3, loops' own time, slot_sum(): return lax.fori_loop(0, live_count, add_block, running)  34.2 us
    all_to_all x3, starting transfers between devices, shards(): lax.all_to_all(grouped, 'cols', split_axis=1, concat_axis=2, tiled=True)  16 us
    dot_general x10, matrix products, add_block(): jnp.dot(solved_piece, factor_piece, preferred_element_type=jnp.float32)  10.8 us
  transfers between devices with their start and end apart: 6, of which 6 were waited for; matrix products, arithmetic and copies ran while one was open for 1% of the time, Pallas kernels for 0%

profile of v1, /device:TPU:2, one launch (start us, length us, event | category | flops | bytes accessed | tf_op | source)
XLA Modules:
  0.0 393.7 jit_solution(16068248112014422649)
XLA Ops:
  6.5 0.9 slice.116
  7.4 1.0 fusion.40
  8.6 30.6 %all_to_all.42 = bf16[64,1,16,256]{3,2,1,0:T(8,128)(2,1)S(1)} all-to-all(bf16[64,1,16,256]{3,2,1,0:T(8,128)(2,1)S(1)} %stack.25), channel_id=1, replica_groups=mesh['rows'=64,'cols'=8] {'rows'}, dimensions={0} | all-to-all | bytes 1048576 | tf_op jit(solution)/shard_map/all_to_all | solution.py:64
  39.2 0.8 copy.11
  40.0 7.1 %all-to-all-start.1 = ((bf16[8,8,16,256]{3,2,0,1:T(8,128)(2,1)}), bf16[8,8,16,256]{3,2,0,1:T(8,128)(2,1)}, u32[]{:S(2)}, u32[]{:S(2)}) async-start(bf16[8,8,16,256]{3,2,0,1:T(8,128)(2,1)} %copy.11), calls=%async_computation.1 | async-start | bytes 1048576 | tf_op jit(solution)/shard_map/all_to_all | solution.py:73
  47.2 0.7 fusion.39
  47.9 1.7 slice_bitcast_fusion
  49.6 16.0 %all-to-all-done.1 = bf16[8,8,16,256]{3,2,0,1:T(8,128)(2,1)} async-done(((bf16[8,8,16,256]{3,2,0,1:T(8,128)(2,1)}), bf16[8,8,16,256]{3,2,0,1:T(8,128)(2,1)}, u32[]{:S(2)}, u32[]{:S(2)}) %all-to-all-start.1) | async-done | bytes 524320 | tf_op jit(solution)/shard_map/all_to_all | solution.py:73
  65.6 1.1 copy.12
  66.8 19.2 %while.42 = (s32[]{:T(128)}, f32[128,256]{1,0:T(8,128)S(1)}, s32[]{:T(128)}, s32[8]{0:T(128)S(1)}, bf16[24,128,256]{2,1,0:T(8,128)(2,1)S(1)}, /*index=5*/bf16[8,...) while((s32[]{:T(128)}, f32[128,256]{1,0:T(8,128)S(1)}, ...), condition=%wide.region_1.2_spmd, body=%wide.region_0.0_spmd.sunk | while | flops 16810028 | bytes 459350 | solution.py:23
  67.6 0.6 dynamic_slice.141
  70.4 1.1 convolution_add_fusion.6
  75.1 1.1 convolution_add_fusion.6
  79.7 1.1 convolution_add_fusion.6
  81.4 0.6 dynamic_slice.141
  84.3 1.1 convolution_add_fusion.6
  86.0 0.7 copy-done.1
  86.7 49.0 %reduce-scatter.4.cloned.1.call-done = f32[16,256]{1,0:T(8,128)} async-done(((f32[128,256]{1,0:T(8,128)}), f32[16,256]{1,0:T(8,128)}) %reduce-scatter.4.cloned.1.call-update) | async-done | bytes 16400 | tf_op jit(solution)/shard_map/reduce_scatter | solution.py:53
  135.8 0.9 fusion.41
  136.7 27.4 %all_to_all.43 = bf16[64,1,16,256]{3,2,1,0:T(8,128)(2,1)S(1)} all-to-all(bf16[64,1,16,256]{3,2,1,0:T(8,128)(2,1)S(1)} %stack.27), channel_id=1, replica_groups=mesh['rows'=64,'cols'=8] {'rows'}, dimensions={0} | all-to-all | bytes 1048576 | tf_op jit(solution)/shard_map/all_to_all | solution.py:64
  164.1 0.8 copy.13
  164.9 4.4 %all-to-all-start.3 = ((bf16[8,8,16,256]{3,2,0,1:T(8,128)(2,1)}), bf16[8,8,16,256]{3,2,0,1:T(8,128)(2,1)S(1)}, u32[]{:S(2)}, u32[]{:S(2)}) async-start(bf16[8,8,16,256]{3,2,0,1:T(8,128)(2,1)} %copy.13), calls=%async_computation.4 | async-start | bytes 1048576 | tf_op jit(solution)/shard_map/all_to_all | solution.py:73
  169.4 18.3 %all-to-all-done.3 = bf16[8,8,16,256]{3,2,0,1:T(8,128)(2,1)S(1)} async-done(((bf16[8,8,16,256]{3,2,0,1:T(8,128)(2,1)}), bf16[8,8,16,256]{3,2,0,1:T(8,128)(2,1)S(1)}, u32[]{:S(2)}, u32[]{:S(2)}) %all-to-all-start.3) | async-done | bytes 524320 | tf_op jit(solution)/shard_map/all_to_all | solution.py:73
  187.8 16.3 %while.43 = (s32[]{:T(128)}, f32[128,256]{1,0:T(8,128)S(1)}, s32[]{:T(128)}, s32[8]{0:T(128)S(1)}, bf16[24,128,256]{2,1,0:T(8,128)(2,1)S(1)}, /*index=5*/bf16[8,...) while((s32[]{:T(128)}, f32[128,256]{1,0:T(8,128)S(1)}, ...), condition=%wide.region_4.5_spmd, body=%wide.region_3.4_spmd.sunk | while | flops 16810028 | bytes 459350 | solution.py:23
  188.4 0.7 dynamic_slice.144
  191.9 1.1 convolution_add_fusion.7
  193.7 0.7 dynamic_slice.144
  197.2 1.1 convolution_add_fusion.7
  198.9 0.7 dynamic_slice.144
  202.4 1.1 convolution_add_fusion.7
  204.1 0.7 copy-done.2
  204.8 56.7 %reduce-scatter.6.cloned.1.call-done = f32[16,256]{1,0:T(8,128)} async-done(((f32[128,256]{1,0:T(8,128)}), f32[16,256]{1,0:T(8,128)}) %reduce-scatter.6.cloned.1.call-update) | async-done | bytes 16400 | tf_op jit(solution)/shard_map/reduce_scatter | solution.py:53
  261.6 0.9 fusion.42
  262.5 27.4 %all_to_all.44 = bf16[64,1,16,256]{3,2,1,0:T(8,128)(2,1)S(1)} all-to-all(bf16[64,1,16,256]{3,2,1,0:T(8,128)(2,1)S(1)} %stack.29), channel_id=1, replica_groups=mesh['rows'=64,'cols'=8] {'rows'}, dimensions={0} | all-to-all | bytes 1048576 | tf_op jit(solution)/shard_map/all_to_all | solution.py:64
  289.9 0.8 copy.15
  290.7 4.4 %all-to-all-start.5 = ((bf16[8,8,16,256]{3,2,0,1:T(8,128)(2,1)}), bf16[8,8,16,256]{3,2,0,1:T(8,128)(2,1)S(1)}, u32[]{:S(2)}, u32[]{:S(2)}) async-start(bf16[8,8,16,256]{3,2,0,1:T(8,128)(2,1)} %copy.15), calls=%async_computation.7 | async-start | bytes 1048576 | tf_op jit(solution)/shard_map/all_to_all | solution.py:73
  295.2 18.3 %all-to-all-done.5 = bf16[8,8,16,256]{3,2,0,1:T(8,128)(2,1)S(1)} async-done(((bf16[8,8,16,256]{3,2,0,1:T(8,128)(2,1)}), bf16[8,8,16,256]{3,2,0,1:T(8,128)(2,1)S(1)}, u32[]{:S(2)}, u32[]{:S(2)}) %all-to-all-start.5) | async-done | bytes 524320 | tf_op jit(solution)/shard_map/all_to_all | solution.py:73
  313.6 15.7 %while.44 = (s32[]{:T(128)}, f32[128,256]{1,0:T(8,128)S(1)}, s32[]{:T(128)}, s32[8]{0:T(128)S(1)}, bf16[24,128,256]{2,1,0:T(8,128)(2,1)S(1)}, /*index=5*/bf16[8,...) while((s32[]{:T(128)}, f32[128,256]{1,0:T(8,128)S(1)}, ...), condition=%wide.region_7.8_spmd, body=%wide.region_6.7_spmd.sunk | while | flops 16810028 | bytes 459350 | solution.py:23
  314.3 0.7 dynamic_slice.147
  317.5 1.1 convolution_add_fusion.8
  319.3 0.7 dynamic_slice.147
  322.5 1.1 convolution_add_fusion.8
  324.3 0.7 dynamic_slice.147
  327.5 1.1 convolution_add_fusion.8
  329.3 0.6 copy-done
  330.0 55.7 %reduce-scatter.8.cloned.1.call-done = f32[16,256]{1,0:T(8,128)} async-done(((f32[128,256]{1,0:T(8,128)}), f32[16,256]{1,0:T(8,128)}) %reduce-scatter.8.cloned.1.call-update) | async-done | bytes 16400 | tf_op jit(solution)/shard_map/reduce_scatter | solution.py:53
  385.7 0.9 convolution_bitcast_fusion
  386.5 0.6 maximum_bitcast_fusion
  (34 shorter events, 1.8 us)
Async XLA Ops:
  8.5 38.6 %copy-start.6 = (s32[3,1,1]{0,2,1:T(1,128)S(1)}, s32[3,1,1]{0,2,1:T(1,128)}, u32[]{:S(2)}) copy-start(s32[3,1,1]{0,2,1:T(1,128)} %param.21) | copy-start | bytes 40
  8.6 39.3 %copy-start.7 = (s32[3,1,1,8]{3,2,1,0:T(1,128)S(1)}, s32[3,1,1,8]{3,2,1,0:T(1,128)}, u32[]{:S(2)}) copy-start(s32[3,1,1,8]{3,2,1,0:T(1,128)} %param.20) | copy-start | bytes 292
  8.6 39.3 %copy-start.3 = (bf16[3,1,1,8,256,256]{5,4,3,2,1,0:T(8,128)(2,1)S(1)}, bf16[3,1,1,8,256,256]{5,4,3,2,1,0:T(8,128)(2,1)}, u32[]{:S(2)}) copy-start(bf16[3,1,1,8,256,256]{5,4,3,2,1,0:T(8,128)(2,1)} %param.18) | copy-start | bytes 9437188
  40.0 25.5 %all-to-all-start.1 = ((bf16[8,8,16,256]{3,2,0,1:T(8,128)(2,1)}), bf16[8,8,16,256]{3,2,0,1:T(8,128)(2,1)}, u32[]{:S(2)}, u32[]{:S(2)}) async-start(bf16[8,8,16,256]{3,2,0,1:T(8,128)(2,1)} %copy.11), calls=%async_computation.1 | async-start | bytes 1048576 | tf_op jit(solution)/shard_map/all_to_all | solution.py:73
  47.1 88.6 %reduce-scatter.4.cloned.1.call-start = ((), (), s32[]{:S(2)}) async-start(), calls=%async_computation.9 | async-start | bytes 147456 | tf_op jit(solution)/shard_map/reduce_scatter | solution.py:53
  66.8 19.9 %copy-start.5 = (f32[4,1,128,256]{3,2,1,0:T(8,128)S(1)}, f32[4,1,128,256]{3,2,1,0:T(8,128)}, u32[]{:S(2)}) copy-start(f32[4,1,128,256]{3,2,1,0:T(8,128)} %param.17) | copy-start | bytes 1572868
  66.8 68.9 %copy-start.4 = (bf16[4,1,256,256]{3,2,1,0:T(8,128)(2,1)S(1)}, bf16[4,1,256,256]{3,2,1,0:T(8,128)(2,1)}, u32[]{:S(2)}) copy-start(bf16[4,1,256,256]{3,2,1,0:T(8,128)(2,1)} %param.19) | copy-start | bytes 1572868
  86.0 0.7 copy-start.1
  164.9 22.8 %all-to-all-start.3 = ((bf16[8,8,16,256]{3,2,0,1:T(8,128)(2,1)}), bf16[8,8,16,256]{3,2,0,1:T(8,128)(2,1)S(1)}, u32[]{:S(2)}, u32[]{:S(2)}) async-start(bf16[8,8,16,256]{3,2,0,1:T(8,128)(2,1)} %copy.13), calls=%async_computation.4 | async-start | bytes 1048576 | tf_op jit(solution)/shard_map/all_to_all | solution.py:73
  169.4 92.2 %reduce-scatter.6.cloned.1.call-start = ((), (), s32[]{:S(2)}) async-start(), calls=%async_computation.10 | async-start | bytes 147456 | tf_op jit(solution)/shard_map/reduce_scatter | solution.py:53
  204.1 0.7 copy-start.2
  290.7 22.7 %all-to-all-start.5 = ((bf16[8,8,16,256]{3,2,0,1:T(8,128)(2,1)}), bf16[8,8,16,256]{3,2,0,1:T(8,128)(2,1)S(1)}, u32[]{:S(2)}, u32[]{:S(2)}) async-start(bf16[8,8,16,256]{3,2,0,1:T(8,128)(2,1)} %copy.15), calls=%async_computation.7 | async-start | bytes 1048576 | tf_op jit(solution)/shard_map/all_to_all | solution.py:73
  295.1 90.5 %reduce-scatter.8.cloned.1.call-start = ((), (), s32[]{:S(2)}) async-start(), calls=%async_computation.11 | async-start | bytes 147456 | tf_op jit(solution)/shard_map/reduce_scatter | solution.py:53
  329.3 0.6 copy-start
Sparse Core Ops, SparseCore 0:
  86.8 48.8 reduce-scatter.3
  204.9 56.5 reduce-scatter.5
  330.1 55.5 reduce-scatter.7
